TPU v7x, 256 devices: a whole 4x4x8 slice. The times are simulated.
256 devices in a mesh: gx: 32 (over z, x), gy: 4 (over y_lo, core), gz: 2 (over y_hi).
Axes of the slice: x: 4, y: 4 (y_hi: 2, y_lo: 2; y = y_hi * 2 + y_lo), z: 8, core: 2. Of those that a mesh axis runs over, the one named last changes fastest.
Arguments:
- coarse_fields: float32 [4, 512, 64, 256], P(None, 'gx', 'gy', 'gz'), may hold values from -6 to 6
- coarse_wind: float32 [3, 512, 64, 256], P(None, 'gx', 'gy', 'gz'), may hold values from -0.4 to 0.4
- fine_fields: float32 [4, 1024, 64, 256], P(None, 'gx', 'gy', 'gz'), may hold values from -6 to 6
- fine_wind: float32 [3, 1024, 64, 256], P(None, 'gx', 'gy', 'gz'), may hold values from -0.4 to 0.4
- fine_owner: int32 [32, 4, 2], P('gx', 'gy', 'gz'), may hold values from 0 to 31, as said below
Outputs:
- coarse_next: float32 [4, 512, 64, 256], P(None, 'gx', 'gy', 'gz')
- fine_next: float32 [4, 1024, 64, 256], P(None, 'gx', 'gy', 'gz')
Inputs may be any that keep to these rules, and one draw needn't show every extreme that they name: `fine_owner`: in each row of fine boxes along the first direction (fixed second and third index), fine box i refines coarse box (i + r) mod 32 for an offset r of that row, so every row names every coarse box once.
All inputs are finite; a program needn't handle non-finite values.
Results may differ from a plain program's by a relative error of at most 0.0003.
Values sent between devices are 32-bit elements; how exact they have to be, the bound alone decides.
A program may use at most 128 MiB of HBM per device.

v0:
```python
import math
import jax
import jax.numpy as jnp
from jax import lax
from jax.sharding import PartitionSpec as P

diffusion = 0.05
section_weights = (1.0 / 3.0, 0.5, 1.0)


def extended(array, sides, width, wrap):
    for axis, dim in sides:
        size, length = (lax.axis_size(axis), array.shape[dim])
        up = [(i, (i + 1) % size) for i in range(size if wrap else size - 1)]
        down = [(j, i) for i, j in up]
        last = lax.slice_in_dim(array, length - width, length, axis=dim)
        first = lax.slice_in_dim(array, 0, width, axis=dim)
        before = lax.ppermute(last, axis, up)
        after = lax.ppermute(first, axis, down)
        array = jnp.concatenate([before, array, after], axis=dim)
    return array


def tendency(padded, velocity):
    center = padded[:, 1:-1, 1:-1, 1:-1]
    along_first = padded[:, 2:, 1:-1, 1:-1] - padded[:, :-2, 1:-1, 1:-1]
    along_second = padded[:, 1:-1, 2:, 1:-1] - padded[:, 1:-1, :-2, 1:-1]
    along_third = padded[:, 1:-1, 1:-1, 2:] - padded[:, 1:-1, 1:-1, :-2]
    beside_all = (
        padded[:, 2:, 1:-1, 1:-1]
        + padded[:, :-2, 1:-1, 1:-1]
        + (padded[:, 1:-1, 2:, 1:-1] + padded[:, 1:-1, :-2, 1:-1])
        + (padded[:, 1:-1, 1:-1, 2:] + padded[:, 1:-1, 1:-1, :-2])
    )
    advect = velocity[0] * along_first + velocity[1] * along_second + velocity[2] * along_third
    return -0.5 * advect + diffusion * (beside_all - 6.0 * center)


def refine(coarse, direction):
    length = coarse.shape[direction]
    low_part = lax.slice_in_dim(coarse, 0, length - 1, axis=direction)
    high_part = lax.slice_in_dim(coarse, 1, length, axis=direction)
    odd_cells = 0.75 * low_part + 0.25 * high_part
    even_cells = 0.25 * low_part + 0.75 * high_part
    paired = jnp.stack((odd_cells, even_cells), axis=direction + 1)
    target = list(coarse.shape)
    target[direction] = 2 * (length - 1)
    return paired.reshape(target)


def coarse_slabs(padded, lead_y, span_y, lead_z, span_z):
    rows_y = jnp.concatenate(
        (padded[:, :, lead_y : lead_y + 2], padded[:, :, lead_y + span_y : lead_y + span_y + 2]),
        axis=2,
    )
    slab_y = rows_y[:, :, :, lead_z : lead_z + span_z + 2]
    rows_z = jnp.concatenate(
        (
            padded[:, :, :, lead_z : lead_z + 2],
            padded[:, :, :, lead_z + span_z : lead_z + span_z + 2],
        ),
        axis=3,
    )
    slab_z = rows_z[:, :, lead_y : lead_y + span_y + 2, :]
    return (slab_y, slab_z)


def slab_faces(slab_y, slab_z):
    wide_y = refine(slab_y, 1)[:, 1:-1]
    low_y = 0.75 * wide_y[:, :, 0] + 0.25 * wide_y[:, :, 1]
    high_y = 0.25 * wide_y[:, :, 2] + 0.75 * wide_y[:, :, 3]
    faces_y = refine(jnp.stack((low_y, high_y), axis=2), 3)[:, :, :, 1:-1]
    wide_z = refine(refine(slab_z, 1)[:, 1:-1], 2)[:, :, 1:-1]
    low_z = 0.75 * wide_z[:, :, :, 0] + 0.25 * wide_z[:, :, :, 1]
    high_z = 0.25 * wide_z[:, :, :, 2] + 0.75 * wide_z[:, :, :, 3]
    faces_z = jnp.stack((low_z, high_z), axis=3)
    return (faces_y, faces_z)


def fine_padded(widened, faces_y, faces_z):
    inner = widened[:, 1:-1]
    middle = jnp.concatenate((faces_z[:, :, :, 0:1], inner, faces_z[:, :, :, 1:2]), axis=3)
    side_low = jnp.pad(faces_y[:, :, 0:1], ((0, 0), (0, 0), (0, 0), (1, 1)))
    side_high = jnp.pad(faces_y[:, :, 1:2], ((0, 0), (0, 0), (0, 0), (1, 1)))
    middle = jnp.concatenate((side_low, middle, side_high), axis=2)
    end_low = jnp.pad(widened[:, 0:1], ((0, 0), (0, 0), (1, 1), (1, 1)))
    end_high = jnp.pad(widened[:, -1:], ((0, 0), (0, 0), (1, 1), (1, 1)))
    return jnp.concatenate((end_low, middle, end_high), axis=1)


def coarsen(fine):
    blocks = fine.reshape(
        fine.shape[0], fine.shape[1] // 2, 2, fine.shape[2] // 2, 2, fine.shape[3] // 2, 2
    )
    return 0.125 * jnp.sum(blocks, axis=(2, 4, 6))


def pack_parts(payload):
    return jnp.concatenate([member.reshape(member.shape[0], -1) for member in payload], axis=1)


def unpack_parts(packed, shapes):
    pieces = []
    cursor = 0
    for target in shapes:
        extent = math.prod(target[1:])
        pieces.append(packed[:, cursor : cursor + extent].reshape(target))
        cursor += extent
    return tuple(pieces)


def send_forward(payload, cycle_size, offset, position):
    shapes = [member.shape for member in payload]
    packed = pack_parts(payload)
    gathered = lax.all_gather(packed[None], "gx", axis=0, tiled=True)
    arrived = lax.dynamic_index_in_dim(
        gathered, (position + offset) % cycle_size, 0, keepdims=False
    )
    return unpack_parts(arrived, shapes)


def send_back(averaged, cycle_size, offset, position):
    packed = averaged.reshape(averaged.shape[0], -1)
    gathered = lax.all_gather(packed[None], "gx", axis=0, tiled=True)
    arrived = lax.dynamic_index_in_dim(
        gathered, (position - offset) % cycle_size, 0, keepdims=False
    )
    return arrived.reshape(averaged.shape)


def shards(coarse_fields, coarse_wind, fine_fields, fine_wind, fine_owner):
    cycle_size = lax.axis_size("gx")
    position = lax.axis_index("gx")
    offset = (fine_owner[0, 0, 0] - position) % cycle_size
    lead_y = coarse_fields.shape[2] // 4
    span_y = coarse_fields.shape[2] // 2
    lead_z = coarse_fields.shape[3] // 4
    span_z = coarse_fields.shape[3] // 2
    coarse_state = coarse_fields
    fine_state = fine_fields
    for fraction in section_weights:
        sides = extended(coarse_state, (("gx", 1), ("gy", 2)), 1, True)
        padded = extended(sides, (("gz", 3),), 1, False)
        coarse_rate = tendency(padded, coarse_wind)
        slab_y, slab_z = coarse_slabs(padded, lead_y, span_y, lead_z, span_z)
        faces_y, faces_z = slab_faces(slab_y, slab_z)
        faces_y, faces_z = send_forward((faces_y, faces_z), cycle_size, offset, position)
        widened = extended(fine_state, (("gx", 1),), 1, True)
        fine_rate = tendency(fine_padded(widened, faces_y, faces_z), fine_wind)
        coarse_state = coarse_fields + fraction * coarse_rate
        fine_state = fine_fields + fraction * fine_rate
    averaged = send_back(coarsen(fine_state), cycle_size, offset, position)
    column = jnp.concatenate(
        (
            coarse_state[:, :, lead_y : lead_y + span_y, :lead_z],
            averaged,
            coarse_state[:, :, lead_y : lead_y + span_y, lead_z + span_z :],
        ),
        axis=3,
    )
    coarse_next = jnp.concatenate(
        (coarse_state[:, :, :lead_y], column, coarse_state[:, :, lead_y + span_y :]), axis=2
    )
    return (coarse_next, fine_state)


def solution(mesh):
    return jax.shard_map(
        shards,
        mesh=mesh,
        in_specs=(
            P(None, "gx", "gy", "gz"),
            P(None, "gx", "gy", "gz"),
            P(None, "gx", "gy", "gz"),
            P(None, "gx", "gy", "gz"),
            P("gx", "gy", "gz"),
        ),
        out_specs=(P(None, "gx", "gy", "gz"), P(None, "gx", "gy", "gz")),
        check_vma=False,
    )
```

profile of v0, /device:TPU:8, one launch (start us, length us, event | category | flops | bytes accessed | tf_op | source)
XLA Modules:
  0.0 454.9 jit_solution(6036083444465853417)
XLA Ops:
  9.5 6.6 %collective-permute-start = (f32[4,1,16,128]{3,2,1,0:T(8,128)S(1)}, f32[4,1,16,128]{3,2,1,0:T(8,128)S(1)}, u32[]{:S(2)}, u32[]{:S(2)}) collective-permute-start(f32[4,1,16,128]{3,2,1,0:T(8,128)S(1)} %get-tuple-element.55), channel_id=1, source_target_pairs={{8,0},{16,8},{24,16},{32,24},{40,32},{48,40},{56,48},{64,56},{72,6... | collective-permute-start | bytes 98312 | tf_op jit(solution)/shard_map/ppermute | solution.py:19
  29.6 6.1 %collective-permute-start.5 = (f32[4,18,18,1]{2,0,3,1:T(4,128)S(1)}, f32[4,18,18,1]{2,0,3,1:T(4,128)S(1)}, u32[]{:S(2)}, u32[]{:S(2)}) collective-permute-start(f32[4,18,18,1]{2,0,3,1:T(4,128)S(1)} %copy.594), channel_id=1, source_target_pairs={{0,1},{2,3},{4,5},{6,7},{8,9},{10,11},{12,13},{14,15},{16,17},{18,... | collective-permute-start | bytes 15560 | tf_op jit(solution)/shard_map/ppermute | solution.py:18
  46.0 2.9 multiply_add_fusion.3
  49.0 5.3 %collective-permute-start.6 = (f32[4,1,16,128]{3,2,1,0:T(8,128)S(1)}, f32[4,1,16,128]{3,2,1,0:T(8,128)S(1)}, u32[]{:S(2)}, u32[]{:S(2)}) collective-permute-start(f32[4,1,16,128]{3,2,1,0:T(8,128)S(1)} %get-tuple-element.54), channel_id=1, source_target_pairs={{8,0},{16,8},{24,16},{32,24},{40,32},{48,40},{56,48},{64,56},{72,6... | collective-permute-start | bytes 98312 | tf_op jit(solution)/shard_map/ppermute | solution.py:19
  61.5 2.3 copy.604
  63.8 2.3 copy.602
  67.4 7.3 %collective-permute-start.11 = (f32[4,18,18,1]{2,0,3,1:T(4,128)}, f32[4,18,18,1]{2,0,3,1:T(4,128)}, u32[]{:S(2)}, u32[]{:S(2)}) collective-permute-start(f32[4,18,18,1]{2,0,3,1:T(4,128)} %copy.604), channel_id=1, source_target_pairs={{0,1},{2,3},{4,5},{6,7},{8,9},{10,11},{12,13},{14,15},{16,17},{18,... | collective-permute-start | bytes 15560 | tf_op jit(solution)/shard_map/ppermute | solution.py:18
  77.0 2.2 copy.642
  90.5 2.2 copy.605
  94.8 5.5 %collective-permute-start.12 = (f32[4,1,16,128]{3,2,1,0:T(8,128)S(1)}, f32[4,1,16,128]{3,2,1,0:T(8,128)S(1)}, u32[]{:S(2)}, u32[]{:S(2)}) collective-permute-start(f32[4,1,16,128]{3,2,1,0:T(8,128)S(1)} %get-tuple-element.52), channel_id=1, source_target_pairs={{8,0},{16,8},{24,16},{32,24},{40,32},{48,40},{56,48},{64,56},{72,6... | collective-permute-start | bytes 98312 | tf_op jit(solution)/shard_map/ppermute | solution.py:19
  107.4 2.3 copy.614
  112.1 6.7 %collective-permute-start.17 = (f32[4,18,18,1]{2,0,3,1:T(4,128)}, f32[4,18,18,1]{2,0,3,1:T(4,128)}, u32[]{:S(2)}, u32[]{:S(2)}) collective-permute-start(f32[4,18,18,1]{2,0,3,1:T(4,128)} %copy.614), channel_id=1, source_target_pairs={{0,1},{2,3},{4,5},{6,7},{8,9},{10,11},{12,13},{14,15},{16,17},{18,... | collective-permute-start | bytes 15560 | tf_op jit(solution)/shard_map/ppermute | solution.py:18
  131.1 5.4 %collective-permute-start.18 = (f32[4,1,16,128]{3,2,1,0:T(8,128)}, f32[4,1,16,128]{3,2,1,0:T(8,128)}, u32[]{:S(2)}, u32[]{:S(2)}) collective-permute-start(f32[4,1,16,128]{3,2,1,0:T(8,128)} %get-tuple-element.19), channel_id=1, source_target_pairs={{8,0},{16,8},{24,16},{32,24},{40,32},{48,40},{56,48},{64,56},{72,6... | collective-permute-start | bytes 98312 | tf_op jit(solution)/shard_map/ppermute | solution.py:19
  139.3 69.0 %all-gather.15.cloned.1.call-done = f32[32,4,9216]{2,1,0:T(4,128)} async-done(((f32[1,4,9216]{2,1,0:T(4,128)}), f32[32,4,9216]{2,1,0:T(4,128)}) %all-gather.15.cloned.1.call-update) | async-done | bytes 4718608 | tf_op jit(solution)/shard_map/all_gather | solution.py:115
  214.2 4.7 %copy.664 = f32[4,32,16,1]{3,2,1,0:T(8,128)S(1)} copy(f32[4,32,16,1]{0,3,2,1:T(1,128)} %get-tuple-element.49) | data formatting | bytes 16384 | tf_op jit(solution)/shard_map/slice | solution.py:82
  218.9 5.6 %copy.665 = f32[4,32,16,1]{3,2,1,0:T(8,128)} copy(f32[4,32,16,1]{0,3,2,1:T(1,128)} %get-tuple-element.50) | data formatting | bytes 16384 | tf_op jit(solution)/shard_map/slice | solution.py:82
  224.5 4.7 %multiply_add_fusion.1 = f32[4,32,16,128]{3,2,1,0:T(8,128)S(1)} fusion(f32[4,32,16,128]{3,2,1,0:T(8,128)S(1)} %copy-done, f32[4,32,16,1]{3,2,1,0:T(8,128)} %copy.665, f32[4,32,16,1]{3,2,1,0:T(8,128)S(1)} %copy.664, f32[4,32,1,130]{3,2,1,0:T(1,128)} %pad.41, f32[4,32,1,130]{3,2,1,0:T(1,128)} %pad.40, f32[4,1,16,128]{3,2,1,0:T(8,128)} %collective-permute-done.18, ...), kind=kLoop, calls=%fused_computation.68 | loop fusion | flops 11534336 | bytes 3098624 | tf_op jit(solution)/shard_map/add | solution.py:151
  230.4 5.3 %collective-permute-start.20 = (f32[4,1,16,128]{3,2,1,0:T(8,128)S(1)}, f32[4,1,16,128]{3,2,1,0:T(8,128)}, u32[]{:S(2)}, u32[]{:S(2)}) collective-permute-start(f32[4,1,16,128]{3,2,1,0:T(8,128)S(1)} %get-tuple-element.17), channel_id=1, source_target_pairs={{8,0},{16,8},{24,16},{32,24},{40,32},{48,40},{56,48},{64,56},{72,6... | collective-permute-start | bytes 98312 | tf_op jit(solution)/shard_map/ppermute | solution.py:19
  237.6 4.7 %copy.668 = f32[4,32,16,1]{3,2,1,0:T(8,128)} copy(f32[4,32,16,1]{0,3,2,1:T(1,128)S(1)} %get-tuple-element.47) | data formatting | bytes 16384 | tf_op jit(solution)/shard_map/slice | solution.py:82
  242.2 4.7 %copy.669 = f32[4,32,16,1]{3,2,1,0:T(8,128)} copy(f32[4,32,16,1]{0,3,2,1:T(1,128)S(1)} %get-tuple-element.48) | data formatting | bytes 16384 | tf_op jit(solution)/shard_map/slice | solution.py:82
  247.5 7.4 %multiply_add_fusion = f32[4,32,16,128]{3,2,1,0:T(8,128)S(1)} fusion(f32[4,32,16,128]{3,2,1,0:T(8,128)S(1)} %copy-done, f32[4,32,16,128]{3,2,1,0:T(8,128)} %copy-done.2, f32[4,32,16,1]{3,2,1,0:T(8,128)} %copy.669, f32[4,32,16,1]{3,2,1,0:T(8,128)} %copy.668, f32[4,32,1,130]{3,2,1,0:T(1,128)} %pad.44, f32[4,32,1,130]{3,2,1,0:T(1,128)S(1)} %pad.39, ...), kind=kLoop, calls=%fused_computation.67 | loop fusion | flops 11534336 | bytes 4147200 | tf_op jit(solution)/shard_map/add | solution.py:151
  255.5 5.5 %collective-permute-start.22 = (f32[4,1,16,128]{3,2,1,0:T(8,128)}, f32[4,1,16,128]{3,2,1,0:T(8,128)}, u32[]{:S(2)}, u32[]{:S(2)}) collective-permute-start(f32[4,1,16,128]{3,2,1,0:T(8,128)} %get-tuple-element.15), channel_id=1, source_target_pairs={{8,0},{16,8},{24,16},{32,24},{40,32},{48,40},{56,48},{64,56},{72,6... | collective-permute-start | bytes 98312 | tf_op jit(solution)/shard_map/ppermute | solution.py:19
  261.1 29.9 %all-gather.13.cloned.1.call-done = f32[32,4,9216]{2,1,0:T(4,128)} async-done(((f32[1,4,9216]{2,1,0:T(4,128)}), f32[32,4,9216]{2,1,0:T(4,128)}) %all-gather.13.cloned.1.call-update) | async-done | bytes 4718608 | tf_op jit(solution)/shard_map/all_gather | solution.py:115
  294.7 2.6 fusion.33
  298.7 5.6 %copy.672 = f32[4,32,16,1]{3,2,1,0:T(8,128)} copy(f32[4,32,16,1]{0,3,2,1:T(1,128)} %get-tuple-element.45) | data formatting | bytes 16384 | tf_op jit(solution)/shard_map/slice | solution.py:82
  304.3 5.6 %copy.673 = f32[4,32,16,1]{3,2,1,0:T(8,128)} copy(f32[4,32,16,1]{0,3,2,1:T(1,128)} %get-tuple-element.46) | data formatting | bytes 16384 | tf_op jit(solution)/shard_map/slice | solution.py:82
  310.0 6.6 %add_add_fusion = f32[4,32,16,128]{3,2,1,0:T(8,128)} fusion(f32[4,32,16,128]{3,2,1,0:T(8,128)S(1)} %copy-done, f32[4,32,16,128]{3,2,1,0:T(8,128)S(1)} %multiply_add_fusion, f32[4,32,16,1]{3,2,1,0:T(8,128)} %copy.673, f32[4,32,16,1]{3,2,1,0:T(8,128)} %copy.672, f32[4,32,1,130]{3,2,1,0:T(1,128)} %pad.47, f32[4,32,1,130]{3,2,1,0:T(1,128)S(1)} %pad.38, ...), kind=kLoop, calls=%fused_computation.66 | loop fusion | flops 11272192 | bytes 4147200 | tf_op jit(solution)/shard_map/add | solution.py:151
  316.6 17.4 %copy.676 = f32[4,32,16,128]{0,3,2,1:T(8,128)} copy(f32[4,32,16,128]{3,2,1,0:T(8,128)} %add_add_fusion) | data formatting | bytes 2097152 | tf_op jit(solution)/shard_map/add | solution.py:151
  334.0 24.2 %reduce_sum.9 = f32[4,16,8,64]{0,3,2,1:T(8,128)} reduce(f32[4,16,2,8,2,64,2]{0,6,5,4,3,2,1:T(2,128)} %bitcast.106, f32[]{:T(128)} %constant.76.clone.1), dimensions={2,4,6}, to_apply=%region_0.1 | reduce | flops 229376 | bytes 1179652 | tf_op jit(solution)/shard_map/reduce_sum | solution.py:95
  358.2 5.0 %broadcast_multiply_fusion = f32[4,16,8,64]{0,3,2,1:T(8,128)} fusion(f32[4,16,8,64]{0,3,2,1:T(8,128)} %reduce_sum.9), kind=kLoop, calls=%fused_computation | loop fusion | flops 32768 | bytes 262144 | tf_op jit(solution)/shard_map/mul | solution.py:95
  363.2 3.6 copy.677
  369.8 76.1 %all-gather.11.cloned.1.call-done = f32[32,4,8192]{2,1,0:T(4,128)} async-done(((f32[1,4,8192]{2,1,0:T(4,128)}), f32[32,4,8192]{2,1,0:T(4,128)}) %all-gather.11.cloned.1.call-update) | async-done | bytes 4194320 | tf_op jit(solution)/shard_map/all_gather | solution.py:124
  (264 shorter events, 93.9 us)
Async XLA Ops:
  7.2 132.1 %all-gather.17.cloned.1.call-start = ((), (), s32[]{:S(2)}) async-start(), calls=%async_computation.3 | async-start | bytes 4866048 | tf_op jit(solution)/shard_map/all_gather | solution.py:115
  8.0 9.9 %collective-permute-start.1 = (f32[4,1,16,128]{3,2,1,0:T(8,128)S(1)}, f32[4,1,16,128]{3,2,1,0:T(8,128)S(1)}, u32[]{:S(2)}, u32[]{:S(2)}) collective-permute-start(f32[4,1,16,128]{3,2,1,0:T(8,128)S(1)} %get-tuple-element.56), channel_id=1, source_target_pairs={{0,8},{8,16},{16,24},{24,32},{32,40},{40,48},{48,56},{56,64},{64,7... | collective-permute-start | bytes 98312 | tf_op jit(solution)/shard_map/ppermute | solution.py:18
  9.5 9.5 %collective-permute-start = (f32[4,1,16,128]{3,2,1,0:T(8,128)S(1)}, f32[4,1,16,128]{3,2,1,0:T(8,128)S(1)}, u32[]{:S(2)}, u32[]{:S(2)}) collective-permute-start(f32[4,1,16,128]{3,2,1,0:T(8,128)S(1)} %get-tuple-element.55), channel_id=1, source_target_pairs={{8,0},{16,8},{24,16},{32,24},{40,32},{48,40},{56,48},{64,56},{72,6... | collective-permute-start | bytes 98312 | tf_op jit(solution)/shard_map/ppermute | solution.py:19
  19.1 1.8 collective-permute-start.2
  19.3 3.5 collective-permute-start.3
  28.3 11.6 %collective-permute-start.4 = (f32[4,18,18,1]{2,0,3,1:T(4,128)S(1)}, f32[4,18,18,1]{2,0,3,1:T(4,128)S(1)}, u32[]{:S(2)}, u32[]{:S(2)}) collective-permute-start(f32[4,18,18,1]{2,0,3,1:T(4,128)S(1)} %copy.592), channel_id=1, source_target_pairs={{1,0},{3,2},{5,4},{7,6},{9,8},{11,10},{13,12},{15,14},{17,16},{19,... | collective-permute-start | bytes 15560 | tf_op jit(solution)/shard_map/ppermute | solution.py:19
  29.6 9.7 %collective-permute-start.5 = (f32[4,18,18,1]{2,0,3,1:T(4,128)S(1)}, f32[4,18,18,1]{2,0,3,1:T(4,128)S(1)}, u32[]{:S(2)}, u32[]{:S(2)}) collective-permute-start(f32[4,18,18,1]{2,0,3,1:T(4,128)S(1)} %copy.594), channel_id=1, source_target_pairs={{0,1},{2,3},{4,5},{6,7},{8,9},{10,11},{12,13},{14,15},{16,17},{18,... | collective-permute-start | bytes 15560 | tf_op jit(solution)/shard_map/ppermute | solution.py:18
  43.7 164.6 %all-gather.15.cloned.1.call-start = ((), (), s32[]{:S(2)}) async-start(), calls=%async_computation.2 | async-start | bytes 4866048 | tf_op jit(solution)/shard_map/all_gather | solution.py:115
  44.0 48.7 %copy-start.5 = (f32[16,16,128]{2,1,0:T(8,128)}, f32[16,16,128]{2,1,0:T(8,128)S(1)}, u32[]{:S(2)}) copy-start(f32[16,16,128]{2,1,0:T(8,128)S(1)} %get-tuple-element.57) | copy-start | bytes 393220
  44.0 48.7 %copy-start.7 = (f32[16,16,128]{2,1,0:T(8,128)}, f32[16,16,128]{2,1,0:T(8,128)S(1)}, u32[]{:S(2)}) copy-start(f32[16,16,128]{2,1,0:T(8,128)S(1)} %get-tuple-element.58) | copy-start | bytes 393220
  44.0 48.7 %copy-start.9 = (f32[16,16,128]{2,1,0:T(8,128)}, f32[16,16,128]{2,1,0:T(8,128)S(1)}, u32[]{:S(2)}) copy-start(f32[16,16,128]{2,1,0:T(8,128)S(1)} %get-tuple-element.59) | copy-start | bytes 393220
  48.9 7.3 %collective-permute-start.7 = (f32[4,1,16,128]{3,2,1,0:T(8,128)S(1)}, f32[4,1,16,128]{3,2,1,0:T(8,128)S(1)}, u32[]{:S(2)}, u32[]{:S(2)}) collective-permute-start(f32[4,1,16,128]{3,2,1,0:T(8,128)S(1)} %get-tuple-element.53), channel_id=1, source_target_pairs={{0,8},{8,16},{16,24},{24,32},{32,40},{40,48},{48,56},{56,64},{64,7... | collective-permute-start | bytes 98312 | tf_op jit(solution)/shard_map/ppermute | solution.py:18
  49.0 7.2 %collective-permute-start.6 = (f32[4,1,16,128]{3,2,1,0:T(8,128)S(1)}, f32[4,1,16,128]{3,2,1,0:T(8,128)S(1)}, u32[]{:S(2)}, u32[]{:S(2)}) collective-permute-start(f32[4,1,16,128]{3,2,1,0:T(8,128)S(1)} %get-tuple-element.54), channel_id=1, source_target_pairs={{8,0},{16,8},{24,16},{32,24},{40,32},{48,40},{56,48},{64,56},{72,6... | collective-permute-start | bytes 98312 | tf_op jit(solution)/shard_map/ppermute | solution.py:19
  56.2 19.0 %copy-start.24 = (f32[4,1,16,128]{3,2,1,0:T(8,128)}, f32[4,1,16,128]{3,2,1,0:T(8,128)S(1)}, u32[]{:S(2)}) copy-start(f32[4,1,16,128]{3,2,1,0:T(8,128)S(1)} %collective-permute-done.6) | copy-start | bytes 98308
  56.3 1.7 collective-permute-start.8
  56.4 3.5 collective-permute-start.9
  66.1 17.2 %collective-permute-start.10 = (f32[4,18,18,1]{2,0,3,1:T(4,128)}, f32[4,18,18,1]{2,0,3,1:T(4,128)}, u32[]{:S(2)}, u32[]{:S(2)}) collective-permute-start(f32[4,18,18,1]{2,0,3,1:T(4,128)} %copy.602), channel_id=1, source_target_pairs={{1,0},{3,2},{5,4},{7,6},{9,8},{11,10},{13,12},{15,14},{17,16},{19,... | collective-permute-start | bytes 15560 | tf_op jit(solution)/shard_map/ppermute | solution.py:19
  67.4 14.6 %collective-permute-start.11 = (f32[4,18,18,1]{2,0,3,1:T(4,128)}, f32[4,18,18,1]{2,0,3,1:T(4,128)}, u32[]{:S(2)}, u32[]{:S(2)}) collective-permute-start(f32[4,18,18,1]{2,0,3,1:T(4,128)} %copy.604), channel_id=1, source_target_pairs={{0,1},{2,3},{4,5},{6,7},{8,9},{10,11},{12,13},{14,15},{16,17},{18,... | collective-permute-start | bytes 15560 | tf_op jit(solution)/shard_map/ppermute | solution.py:18
  88.9 202.1 %all-gather.13.cloned.1.call-start = ((), (), s32[]{:S(2)}) async-start(), calls=%async_computation.1 | async-start | bytes 4866048 | tf_op jit(solution)/shard_map/all_gather | solution.py:115
  94.7 7.5 %collective-permute-start.13 = (f32[4,1,16,128]{3,2,1,0:T(8,128)S(1)}, f32[4,1,16,128]{3,2,1,0:T(8,128)S(1)}, u32[]{:S(2)}, u32[]{:S(2)}) collective-permute-start(f32[4,1,16,128]{3,2,1,0:T(8,128)S(1)} %get-tuple-element.51), channel_id=1, source_target_pairs={{0,8},{8,16},{16,24},{24,32},{32,40},{40,48},{48,56},{56,64},{64,7... | collective-permute-start | bytes 98312 | tf_op jit(solution)/shard_map/ppermute | solution.py:18
  94.8 7.4 %collective-permute-start.12 = (f32[4,1,16,128]{3,2,1,0:T(8,128)S(1)}, f32[4,1,16,128]{3,2,1,0:T(8,128)S(1)}, u32[]{:S(2)}, u32[]{:S(2)}) collective-permute-start(f32[4,1,16,128]{3,2,1,0:T(8,128)S(1)} %get-tuple-element.52), channel_id=1, source_target_pairs={{8,0},{16,8},{24,16},{32,24},{40,32},{48,40},{56,48},{64,56},{72,6... | collective-permute-start | bytes 98312 | tf_op jit(solution)/shard_map/ppermute | solution.py:19
  102.3 1.7 collective-permute-start.14
  102.4 3.6 collective-permute-start.15
  110.8 13.6 %collective-permute-start.16 = (f32[4,18,18,1]{2,0,3,1:T(4,128)}, f32[4,18,18,1]{2,0,3,1:T(4,128)S(1)}, u32[]{:S(2)}, u32[]{:S(2)}) collective-permute-start(f32[4,18,18,1]{2,0,3,1:T(4,128)} %copy.612), channel_id=1, source_target_pairs={{1,0},{3,2},{5,4},{7,6},{9,8},{11,10},{13,12},{15,14},{17,16},{19,... | collective-permute-start | bytes 15560 | tf_op jit(solution)/shard_map/ppermute | solution.py:19
  112.1 10.9 %collective-permute-start.17 = (f32[4,18,18,1]{2,0,3,1:T(4,128)}, f32[4,18,18,1]{2,0,3,1:T(4,128)}, u32[]{:S(2)}, u32[]{:S(2)}) collective-permute-start(f32[4,18,18,1]{2,0,3,1:T(4,128)} %copy.614), channel_id=1, source_target_pairs={{0,1},{2,3},{4,5},{6,7},{8,9},{10,11},{12,13},{14,15},{16,17},{18,... | collective-permute-start | bytes 15560 | tf_op jit(solution)/shard_map/ppermute | solution.py:18
  130.0 315.8 %all-gather.11.cloned.1.call-start = ((), (), s32[]{:S(2)}) async-start(), calls=%async_computation | async-start | bytes 4325376 | tf_op jit(solution)/shard_map/all_gather | solution.py:124
  130.7 93.8 %collective-permute-start.19 = (f32[4,1,16,128]{3,2,1,0:T(8,128)}, f32[4,1,16,128]{3,2,1,0:T(8,128)}, u32[]{:S(2)}, u32[]{:S(2)}) collective-permute-start(f32[4,1,16,128]{3,2,1,0:T(8,128)} %get-tuple-element.18), channel_id=1, source_target_pairs={{0,8},{8,16},{16,24},{24,32},{32,40},{40,48},{48,56},{56,64},{64,7... | collective-permute-start | bytes 98312 | tf_op jit(solution)/shard_map/ppermute | solution.py:18
  131.1 93.4 %collective-permute-start.18 = (f32[4,1,16,128]{3,2,1,0:T(8,128)}, f32[4,1,16,128]{3,2,1,0:T(8,128)}, u32[]{:S(2)}, u32[]{:S(2)}) collective-permute-start(f32[4,1,16,128]{3,2,1,0:T(8,128)} %get-tuple-element.19), channel_id=1, source_target_pairs={{8,0},{16,8},{24,16},{32,24},{40,32},{48,40},{56,48},{64,56},{72,6... | collective-permute-start | bytes 98312 | tf_op jit(solution)/shard_map/ppermute | solution.py:19
  230.2 16.7 %collective-permute-start.21 = (f32[4,1,16,128]{3,2,1,0:T(8,128)S(1)}, f32[4,1,16,128]{3,2,1,0:T(8,128)S(1)}, u32[]{:S(2)}, u32[]{:S(2)}) collective-permute-start(f32[4,1,16,128]{3,2,1,0:T(8,128)S(1)} %get-tuple-element.16), channel_id=1, source_target_pairs={{0,8},{8,16},{16,24},{24,32},{32,40},{40,48},{48,56},{56,64},{64,7... | collective-permute-start | bytes 98312 | tf_op jit(solution)/shard_map/ppermute | solution.py:18
  230.4 17.1 %collective-permute-start.20 = (f32[4,1,16,128]{3,2,1,0:T(8,128)S(1)}, f32[4,1,16,128]{3,2,1,0:T(8,128)}, u32[]{:S(2)}, u32[]{:S(2)}) collective-permute-start(f32[4,1,16,128]{3,2,1,0:T(8,128)S(1)} %get-tuple-element.17), channel_id=1, source_target_pairs={{8,0},{16,8},{24,16},{32,24},{40,32},{48,40},{56,48},{64,56},{72,6... | collective-permute-start | bytes 98312 | tf_op jit(solution)/shard_map/ppermute | solution.py:19
  255.5 54.4 %collective-permute-start.23 = (f32[4,1,16,128]{3,2,1,0:T(8,128)}, f32[4,1,16,128]{3,2,1,0:T(8,128)}, u32[]{:S(2)}, u32[]{:S(2)}) collective-permute-start(f32[4,1,16,128]{3,2,1,0:T(8,128)} %get-tuple-element.14), channel_id=1, source_target_pairs={{0,8},{8,16},{16,24},{24,32},{32,40},{40,48},{48,56},{56,64},{64,7... | collective-permute-start | bytes 98312 | tf_op jit(solution)/shard_map/ppermute | solution.py:18
  255.5 54.4 %collective-permute-start.22 = (f32[4,1,16,128]{3,2,1,0:T(8,128)}, f32[4,1,16,128]{3,2,1,0:T(8,128)}, u32[]{:S(2)}, u32[]{:S(2)}) collective-permute-start(f32[4,1,16,128]{3,2,1,0:T(8,128)} %get-tuple-element.15), channel_id=1, source_target_pairs={{8,0},{16,8},{24,16},{32,24},{40,32},{48,40},{56,48},{64,56},{72,6... | collective-permute-start | bytes 98312 | tf_op jit(solution)/shard_map/ppermute | solution.py:19
  (25 other events, 194.5 us)
Sparse Core Ops, SparseCore 0:
  43.8 82.2 all-gather.16
  128.7 79.5 all-gather.14
  210.9 80.0 all-gather.12
  366.9 78.9 all-gather.10
where the time goes:
time: 464 us; the launch traced here: 455 us
  waiting for transfers between devices  189 us (41%)
  local copies, waits for them, and re-layouts  119 us (26%)
  other arithmetic  68.2 us (15%)
  starting transfers between devices  62.3 us (13%)
  between operations  15.8 us (3%)
    all_gather x3, waiting for transfers between devices, send_forward(): gathered = lax.all_gather(packed[None], 'gx', axis=0, tiled=True)  98.9 us
    all_gather x1, waiting for transfers between devices, send_back(): gathered = lax.all_gather(packed[None], 'gx', axis=0, tiled=True)  76.1 us
    ppermute x12, starting transfers between devices, extended(): after = lax.ppermute(first, axis, down)  37.8 us
    reduce_sum x1, other arithmetic, coarsen(): return 0.125 * jnp.sum(blocks, axis=(2, 4, 6))  24.2 us
    ppermute x12, starting transfers between devices, extended(): before = lax.ppermute(last, axis, up)  23.9 us
    slice x6, local copies, waits for them, and re-layouts, fine_padded(): faces_z[:, :, :, 0:1]  19.2 us
    add x3, other arithmetic, shards(): fine_state = fine_fields + fraction * fine_rate  18.7 us
    add x1, local copies, waits for them, and re-layouts, shards(): fine_state = fine_fields + fraction * fine_rate  17.4 us
  transfers between devices with their start and end apart: 28, of which 12 were waited for; matrix products, arithmetic and copies ran while one was open for 26% of the time, Pallas kernels for 0%

commit v1 on v0

--- a/solution.py
+++ b/solution.py
@@ -121,7 +121,10 @@
 
 def send_back(averaged, cycle_size, offset, position):
     packed = averaged.reshape(averaged.shape[0], -1)
-    gathered = lax.all_gather(packed[None], "gx", axis=0, tiled=True)
+    own_rows = packed[None]
+    gathered = jnp.concatenate(
+        lax.all_to_all(jnp.stack(lax.psum(1, axis_name="gx") * [own_rows], axis=0), "gx", 0, 0), 0
+    )
     arrived = lax.dynamic_index_in_dim(
         gathered, (position - offset) % cycle_size, 0, keepdims=False
     )

time: 464 us -> 489 us (1.054)
  waiting for transfers between devices: 189 us -> 208 us
    all_to_all x0 -> x1, waiting for transfers between devices: none -> 89.4 us  [send_back(): lax.all_to_all(jnp.stack(lax.psum(1, axis_name='gx') * [own_rows], axis=0...]
    all_gather x1 -> x0, waiting for transfers between devices: 76.1 us -> none  [send_back(): gathered = lax.all_gather(packed[None], 'gx', axis=0, tiled=True)]
    all_to_all x0 -> x1, starting transfers between devices: none -> 5.7 us  [send_back(): lax.all_to_all(jnp.stack(lax.psum(1, axis_name='gx') * [own_rows], axis=0...]
    all_gather x3, waiting for transfers between devices: 98.9 us -> 104 us  [send_forward(): gathered = lax.all_gather(packed[None], 'gx', axis=0, tiled=True)]
  transfers between devices with their start and end apart: 28 -> 28, of which waited for: 12 -> 14; matrix products, arithmetic and copies ran while one was open for 26% -> 24% of each run, Pallas kernels for 0% -> 0%
where the time goes in v1:
time: 489 us; the launch traced here: 480 us
  waiting for transfers between devices  208 us (43%)
  local copies, waits for them, and re-layouts  122 us (25%)
  other arithmetic  67.6 us (14%)
  starting transfers between devices  67 us (14%)
  between operations  15.9 us (3%)
    all_gather x3, waiting for transfers between devices, send_forward(): gathered = lax.all_gather(packed[None], 'gx', axis=0, tiled=True)  104 us
    all_to_all x1, waiting for transfers between devices, send_back(): lax.all_to_all(jnp.stack(lax.psum(1, axis_name='gx') * [own_rows], axis=0...  89.4 us
    ppermute x12, starting transfers between devices, extended(): after = lax.ppermute(first, axis, down)  38.7 us
    reduce_sum x1, other arithmetic, coarsen(): return 0.125 * jnp.sum(blocks, axis=(2, 4, 6))  24.2 us
    ppermute x12, starting transfers between devices, extended(): before = lax.ppermute(last, axis, up)  21.9 us
    slice x6, local copies, waits for them, and re-layouts, fine_padded(): faces_z[:, :, :, 0:1]  19.2 us
    add x3, other arithmetic, shards(): fine_state = fine_fields + fraction * fine_rate  18.9 us
    add x1, local copies, waits for them, and re-layouts, shards(): fine_state = fine_fields + fraction * fine_rate  17.4 us
  transfers between devices with their start and end apart: 28, of which 14 were waited for; matrix products, arithmetic and copies ran while one was open for 24% of the time, Pallas kernels for 0%

profile of v1, /device:TPU:8, one launch (start us, length us, event | category | flops | bytes accessed | tf_op | source)
XLA Modules:
  0.0 480.2 jit_solution(2495319471081327119)
XLA Ops:
  9.5 6.6 %collective-permute-start = (f32[4,1,16,128]{3,2,1,0:T(8,128)S(1)}, f32[4,1,16,128]{3,2,1,0:T(8,128)S(1)}, u32[]{:S(2)}, u32[]{:S(2)}) collective-permute-start(f32[4,1,16,128]{3,2,1,0:T(8,128)S(1)} %get-tuple-element.55), channel_id=1, source_target_pairs={{8,0},{16,8},{24,16},{32,24},{40,32},{48,40},{56,48},{64,56},{72,6... | collective-permute-start | bytes 98312 | tf_op jit(solution)/shard_map/ppermute | solution.py:19
  26.4 2.3 copy.594
  31.2 6.0 %collective-permute-start.5 = (f32[4,18,18,1]{2,0,3,1:T(4,128)}, f32[4,18,18,1]{2,0,3,1:T(4,128)S(1)}, u32[]{:S(2)}, u32[]{:S(2)}) collective-permute-start(f32[4,18,18,1]{2,0,3,1:T(4,128)} %copy.594), channel_id=1, source_target_pairs={{0,1},{2,3},{4,5},{6,7},{8,9},{10,11},{12,13},{14,15},{16,17},{18,... | collective-permute-start | bytes 15560 | tf_op jit(solution)/shard_map/ppermute | solution.py:18
  50.6 5.3 %collective-permute-start.6 = (f32[4,1,16,128]{3,2,1,0:T(8,128)S(1)}, f32[4,1,16,128]{3,2,1,0:T(8,128)S(1)}, u32[]{:S(2)}, u32[]{:S(2)}) collective-permute-start(f32[4,1,16,128]{3,2,1,0:T(8,128)S(1)} %get-tuple-element.54), channel_id=1, source_target_pairs={{8,0},{16,8},{24,16},{32,24},{40,32},{48,40},{56,48},{64,56},{72,6... | collective-permute-start | bytes 98312 | tf_op jit(solution)/shard_map/ppermute | solution.py:19
  63.5 2.3 copy.604
  68.2 6.0 %collective-permute-start.11 = (f32[4,18,18,1]{2,0,3,1:T(4,128)}, f32[4,18,18,1]{2,0,3,1:T(4,128)S(1)}, u32[]{:S(2)}, u32[]{:S(2)}) collective-permute-start(f32[4,18,18,1]{2,0,3,1:T(4,128)} %copy.604), channel_id=1, source_target_pairs={{0,1},{2,3},{4,5},{6,7},{8,9},{10,11},{12,13},{14,15},{16,17},{18,... | collective-permute-start | bytes 15560 | tf_op jit(solution)/shard_map/ppermute | solution.py:18
  87.2 5.9 %collective-permute-start.12 = (f32[4,1,16,128]{3,2,1,0:T(8,128)S(1)}, f32[4,1,16,128]{3,2,1,0:T(8,128)S(1)}, u32[]{:S(2)}, u32[]{:S(2)}) collective-permute-start(f32[4,1,16,128]{3,2,1,0:T(8,128)S(1)} %get-tuple-element.52), channel_id=1, source_target_pairs={{8,0},{16,8},{24,16},{32,24},{40,32},{48,40},{56,48},{64,56},{72,6... | collective-permute-start | bytes 98312 | tf_op jit(solution)/shard_map/ppermute | solution.py:19
  103.8 6.1 %collective-permute-start.17 = (f32[4,18,18,1]{2,0,3,1:T(4,128)S(1)}, f32[4,18,18,1]{2,0,3,1:T(4,128)S(1)}, u32[]{:S(2)}, u32[]{:S(2)}) collective-permute-start(f32[4,18,18,1]{2,0,3,1:T(4,128)S(1)} %copy.614), channel_id=1, source_target_pairs={{0,1},{2,3},{4,5},{6,7},{8,9},{10,11},{12,13},{14,15},{16,17},{18,... | collective-permute-start | bytes 15560 | tf_op jit(solution)/shard_map/ppermute | solution.py:18
  112.2 2.2 copy.625
  124.9 5.9 %collective-permute-start.18 = (f32[4,1,16,128]{3,2,1,0:T(8,128)}, f32[4,1,16,128]{3,2,1,0:T(8,128)}, u32[]{:S(2)}, u32[]{:S(2)}) collective-permute-start(f32[4,1,16,128]{3,2,1,0:T(8,128)} %get-tuple-element.19), channel_id=1, source_target_pairs={{8,0},{16,8},{24,16},{32,24},{40,32},{48,40},{56,48},{64,56},{72,6... | collective-permute-start | bytes 98312 | tf_op jit(solution)/shard_map/ppermute | solution.py:19
  131.4 2.0 slice_bitcast_fusion.2
  133.4 75.9 %all-gather.12.cloned.1.call-done = f32[32,4,9216]{2,1,0:T(4,128)} async-done(((f32[1,4,9216]{2,1,0:T(4,128)}), f32[32,4,9216]{2,1,0:T(4,128)}) %all-gather.12.cloned.1.call-update) | async-done | bytes 4718608 | tf_op jit(solution)/shard_map/all_gather | solution.py:115
  215.9 4.7 copy.664
  220.6 5.6 %copy.665 = f32[4,32,16,1]{3,2,1,0:T(8,128)} copy(f32[4,32,16,1]{0,3,2,1:T(1,128)} %get-tuple-element.50) | data formatting | bytes 16384 | tf_op jit(solution)/shard_map/slice | solution.py:82
  226.2 4.7 multiply_add_fusion.1
  232.2 5.3 %collective-permute-start.20 = (f32[4,1,16,128]{3,2,1,0:T(8,128)S(1)}, f32[4,1,16,128]{3,2,1,0:T(8,128)}, u32[]{:S(2)}, u32[]{:S(2)}) collective-permute-start(f32[4,1,16,128]{3,2,1,0:T(8,128)S(1)} %get-tuple-element.17), channel_id=1, source_target_pairs={{8,0},{16,8},{24,16},{32,24},{40,32},{48,40},{56,48},{64,56},{72,6... | collective-permute-start | bytes 98312 | tf_op jit(solution)/shard_map/ppermute | solution.py:19
  241.0 4.7 copy.668
  245.6 4.7 copy.669
  250.3 7.5 %multiply_add_fusion = f32[4,32,16,128]{3,2,1,0:T(8,128)S(1)} fusion(f32[4,32,16,128]{3,2,1,0:T(8,128)S(1)} %copy-done, f32[4,32,16,128]{3,2,1,0:T(8,128)} %copy-done.2, f32[4,32,16,1]{3,2,1,0:T(8,128)} %copy.669, f32[4,32,16,1]{3,2,1,0:T(8,128)} %copy.668, f32[4,32,1,130]{3,2,1,0:T(1,128)} %pad.44, f32[4,32,1,130]{3,2,1,0:T(1,128)} %pad.39, ...), kind=kLoop, calls=%fused_computation.67 | loop fusion | flops 11534336 | bytes 4147200 | tf_op jit(solution)/shard_map/add | solution.py:154
  258.5 5.6 %collective-permute-start.22 = (f32[4,1,16,128]{3,2,1,0:T(8,128)}, f32[4,1,16,128]{3,2,1,0:T(8,128)}, u32[]{:S(2)}, u32[]{:S(2)}) collective-permute-start(f32[4,1,16,128]{3,2,1,0:T(8,128)} %get-tuple-element.15), channel_id=1, source_target_pairs={{8,0},{16,8},{24,16},{32,24},{40,32},{48,40},{56,48},{64,56},{72,6... | collective-permute-start | bytes 98312 | tf_op jit(solution)/shard_map/ppermute | solution.py:19
  264.0 28.3 %all-gather.10.cloned.1.call-done = f32[32,4,9216]{2,1,0:T(4,128)} async-done(((f32[1,4,9216]{2,1,0:T(4,128)}), f32[32,4,9216]{2,1,0:T(4,128)}) %all-gather.10.cloned.1.call-update) | async-done | bytes 4718608 | tf_op jit(solution)/shard_map/all_gather | solution.py:115
  296.6 2.6 fusion.33
  302.4 5.6 %copy.672 = f32[4,32,16,1]{3,2,1,0:T(8,128)} copy(f32[4,32,16,1]{0,3,2,1:T(1,128)} %get-tuple-element.45) | data formatting | bytes 16384 | tf_op jit(solution)/shard_map/slice | solution.py:82
  308.0 5.6 %copy.673 = f32[4,32,16,1]{3,2,1,0:T(8,128)} copy(f32[4,32,16,1]{0,3,2,1:T(1,128)} %get-tuple-element.46) | data formatting | bytes 16384 | tf_op jit(solution)/shard_map/slice | solution.py:82
  313.6 6.7 %add_add_fusion = f32[4,32,16,128]{3,2,1,0:T(8,128)} fusion(f32[4,32,16,128]{3,2,1,0:T(8,128)S(1)} %copy-done, f32[4,32,16,128]{3,2,1,0:T(8,128)S(1)} %multiply_add_fusion, f32[4,32,16,1]{3,2,1,0:T(8,128)} %copy.673, f32[4,32,16,1]{3,2,1,0:T(8,128)} %copy.672, f32[4,32,1,130]{3,2,1,0:T(1,128)} %pad.47, f32[4,32,1,130]{3,2,1,0:T(1,128)} %pad.38, ...), kind=kLoop, calls=%fused_computation.66 | loop fusion | flops 11272192 | bytes 4147200 | tf_op jit(solution)/shard_map/add | solution.py:154
  320.3 17.4 %copy.676 = f32[4,32,16,128]{0,3,2,1:T(8,128)} copy(f32[4,32,16,128]{3,2,1,0:T(8,128)} %add_add_fusion) | data formatting | bytes 2097152 | tf_op jit(solution)/shard_map/add | solution.py:154
  337.7 24.2 %reduce_sum.9 = f32[4,16,8,64]{0,3,2,1:T(8,128)} reduce(f32[4,16,2,8,2,64,2]{0,6,5,4,3,2,1:T(2,128)} %bitcast.106, f32[]{:T(128)} %constant.77.clone.1), dimensions={2,4,6}, to_apply=%region_0.1 | reduce | flops 229376 | bytes 1179652 | tf_op jit(solution)/shard_map/reduce_sum | solution.py:95
  361.9 5.0 %broadcast_multiply_fusion = f32[4,16,8,64]{0,3,2,1:T(8,128)} fusion(f32[4,16,8,64]{0,3,2,1:T(8,128)} %reduce_sum.9), kind=kLoop, calls=%fused_computation | loop fusion | flops 32768 | bytes 262144 | tf_op jit(solution)/shard_map/mul | solution.py:95
  366.8 2.8 copy.677
  369.7 3.0 stack.183
  372.6 5.7 %all-to-all-start = ((f32[32,1,4,8192]{3,2,1,0:T(4,128)}), f32[32,1,4,8192]{3,2,1,0:T(4,128)}, u32[]{:S(2)}, u32[]{:S(2)}) async-start(f32[32,1,4,8192]{3,2,1,0:T(4,128)} %stack.183), calls=%async_computation | async-start | bytes 8388608 | tf_op jit(solution)/shard_map/all_to_all | solution.py:126
  381.6 89.4 %all-to-all-done = f32[32,1,4,8192]{3,2,1,0:T(4,128)} async-done(((f32[32,1,4,8192]{3,2,1,0:T(4,128)}), f32[32,1,4,8192]{3,2,1,0:T(4,128)}, u32[]{:S(2)}, u32[]{:S(2)}) %all-to-all-start) | async-done | bytes 4194336 | tf_op jit(solution)/shard_map/all_to_all | solution.py:126
  (266 shorter events, 98.6 us)
Async XLA Ops:
  7.2 126.2 %all-gather.14.cloned.1.call-start = ((), (), s32[]{:S(2)}) async-start(), calls=%async_computation.3 | async-start | bytes 4866048 | tf_op jit(solution)/shard_map/all_gather | solution.py:115
  8.0 9.9 %collective-permute-start.1 = (f32[4,1,16,128]{3,2,1,0:T(8,128)S(1)}, f32[4,1,16,128]{3,2,1,0:T(8,128)S(1)}, u32[]{:S(2)}, u32[]{:S(2)}) collective-permute-start(f32[4,1,16,128]{3,2,1,0:T(8,128)S(1)} %get-tuple-element.56), channel_id=1, source_target_pairs={{0,8},{8,16},{16,24},{24,32},{32,40},{40,48},{48,56},{56,64},{64,7... | collective-permute-start | bytes 98312 | tf_op jit(solution)/shard_map/ppermute | solution.py:18
  9.5 10.1 %collective-permute-start = (f32[4,1,16,128]{3,2,1,0:T(8,128)S(1)}, f32[4,1,16,128]{3,2,1,0:T(8,128)S(1)}, u32[]{:S(2)}, u32[]{:S(2)}) collective-permute-start(f32[4,1,16,128]{3,2,1,0:T(8,128)S(1)} %get-tuple-element.55), channel_id=1, source_target_pairs={{8,0},{16,8},{24,16},{32,24},{40,32},{48,40},{56,48},{64,56},{72,6... | collective-permute-start | bytes 98312 | tf_op jit(solution)/shard_map/ppermute | solution.py:19
  20.3 1.8 collective-permute-start.2
  20.4 3.5 collective-permute-start.3
  29.9 11.6 %collective-permute-start.4 = (f32[4,18,18,1]{2,0,3,1:T(4,128)}, f32[4,18,18,1]{2,0,3,1:T(4,128)S(1)}, u32[]{:S(2)}, u32[]{:S(2)}) collective-permute-start(f32[4,18,18,1]{2,0,3,1:T(4,128)} %copy.592), channel_id=1, source_target_pairs={{1,0},{3,2},{5,4},{7,6},{9,8},{11,10},{13,12},{15,14},{17,16},{19,... | collective-permute-start | bytes 15560 | tf_op jit(solution)/shard_map/ppermute | solution.py:19
  31.2 9.8 %collective-permute-start.5 = (f32[4,18,18,1]{2,0,3,1:T(4,128)}, f32[4,18,18,1]{2,0,3,1:T(4,128)S(1)}, u32[]{:S(2)}, u32[]{:S(2)}) collective-permute-start(f32[4,18,18,1]{2,0,3,1:T(4,128)} %copy.594), channel_id=1, source_target_pairs={{0,1},{2,3},{4,5},{6,7},{8,9},{10,11},{12,13},{14,15},{16,17},{18,... | collective-permute-start | bytes 15560 | tf_op jit(solution)/shard_map/ppermute | solution.py:18
  45.4 164.0 %all-gather.12.cloned.1.call-start = ((), (), s32[]{:S(2)}) async-start(), calls=%async_computation.2 | async-start | bytes 4866048 | tf_op jit(solution)/shard_map/all_gather | solution.py:115
  47.4 37.8 %copy-start.6 = (f32[16,16,128]{2,1,0:T(8,128)}, f32[16,16,128]{2,1,0:T(8,128)S(1)}, u32[]{:S(2)}) copy-start(f32[16,16,128]{2,1,0:T(8,128)S(1)} %get-tuple-element.57) | copy-start | bytes 393220
  50.5 7.3 %collective-permute-start.7 = (f32[4,1,16,128]{3,2,1,0:T(8,128)S(1)}, f32[4,1,16,128]{3,2,1,0:T(8,128)S(1)}, u32[]{:S(2)}, u32[]{:S(2)}) collective-permute-start(f32[4,1,16,128]{3,2,1,0:T(8,128)S(1)} %get-tuple-element.53), channel_id=1, source_target_pairs={{0,8},{8,16},{16,24},{24,32},{32,40},{40,48},{48,56},{56,64},{64,7... | collective-permute-start | bytes 98312 | tf_op jit(solution)/shard_map/ppermute | solution.py:18
  50.6 7.3 %collective-permute-start.6 = (f32[4,1,16,128]{3,2,1,0:T(8,128)S(1)}, f32[4,1,16,128]{3,2,1,0:T(8,128)S(1)}, u32[]{:S(2)}, u32[]{:S(2)}) collective-permute-start(f32[4,1,16,128]{3,2,1,0:T(8,128)S(1)} %get-tuple-element.54), channel_id=1, source_target_pairs={{8,0},{16,8},{24,16},{32,24},{40,32},{48,40},{56,48},{64,56},{72,6... | collective-permute-start | bytes 98312 | tf_op jit(solution)/shard_map/ppermute | solution.py:19
  57.9 1.7 collective-permute-start.8
  58.0 3.5 collective-permute-start.9
  66.9 12.2 %collective-permute-start.10 = (f32[4,18,18,1]{2,0,3,1:T(4,128)}, f32[4,18,18,1]{2,0,3,1:T(4,128)S(1)}, u32[]{:S(2)}, u32[]{:S(2)}) collective-permute-start(f32[4,18,18,1]{2,0,3,1:T(4,128)} %copy.602), channel_id=1, source_target_pairs={{1,0},{3,2},{5,4},{7,6},{9,8},{11,10},{13,12},{15,14},{17,16},{19,... | collective-permute-start | bytes 15560 | tf_op jit(solution)/shard_map/ppermute | solution.py:19
  68.2 10.3 %collective-permute-start.11 = (f32[4,18,18,1]{2,0,3,1:T(4,128)}, f32[4,18,18,1]{2,0,3,1:T(4,128)S(1)}, u32[]{:S(2)}, u32[]{:S(2)}) collective-permute-start(f32[4,18,18,1]{2,0,3,1:T(4,128)} %copy.604), channel_id=1, source_target_pairs={{0,1},{2,3},{4,5},{6,7},{8,9},{10,11},{12,13},{14,15},{16,17},{18,... | collective-permute-start | bytes 15560 | tf_op jit(solution)/shard_map/ppermute | solution.py:18
  83.6 208.7 %all-gather.10.cloned.1.call-start = ((), (), s32[]{:S(2)}) async-start(), calls=%async_computation.1 | async-start | bytes 4866048 | tf_op jit(solution)/shard_map/all_gather | solution.py:115
  87.2 7.8 %collective-permute-start.13 = (f32[4,1,16,128]{3,2,1,0:T(8,128)S(1)}, f32[4,1,16,128]{3,2,1,0:T(8,128)S(1)}, u32[]{:S(2)}, u32[]{:S(2)}) collective-permute-start(f32[4,1,16,128]{3,2,1,0:T(8,128)S(1)} %get-tuple-element.51), channel_id=1, source_target_pairs={{0,8},{8,16},{16,24},{24,32},{32,40},{40,48},{48,56},{56,64},{64,7... | collective-permute-start | bytes 98312 | tf_op jit(solution)/shard_map/ppermute | solution.py:18
  87.2 7.9 %collective-permute-start.12 = (f32[4,1,16,128]{3,2,1,0:T(8,128)S(1)}, f32[4,1,16,128]{3,2,1,0:T(8,128)S(1)}, u32[]{:S(2)}, u32[]{:S(2)}) collective-permute-start(f32[4,1,16,128]{3,2,1,0:T(8,128)S(1)} %get-tuple-element.52), channel_id=1, source_target_pairs={{8,0},{16,8},{24,16},{32,24},{40,32},{48,40},{56,48},{64,56},{72,6... | collective-permute-start | bytes 98312 | tf_op jit(solution)/shard_map/ppermute | solution.py:19
  94.9 15.4 %copy-start.14 = (f32[4,1,16,128]{3,2,1,0:T(8,128)}, f32[4,1,16,128]{3,2,1,0:T(8,128)S(1)}, u32[]{:S(2)}) copy-start(f32[4,1,16,128]{3,2,1,0:T(8,128)S(1)} %collective-permute-done.13) | copy-start | bytes 98308
  95.2 15.2 %copy-start.15 = (f32[4,1,16,128]{3,2,1,0:T(8,128)}, f32[4,1,16,128]{3,2,1,0:T(8,128)S(1)}, u32[]{:S(2)}) copy-start(f32[4,1,16,128]{3,2,1,0:T(8,128)S(1)} %collective-permute-done.12) | copy-start | bytes 98308
  95.2 1.7 collective-permute-start.14
  95.3 3.5 collective-permute-start.15
  98.8 11.5 %copy-start.8 = (f32[4,18,1,128]{3,2,1,0:T(1,128)}, f32[4,18,1,128]{3,2,1,0:T(1,128)S(1)}, u32[]{:S(2)}) copy-start(f32[4,18,1,128]{3,2,1,0:T(1,128)S(1)} %copy.609) | copy-start | bytes 110596
  102.5 15.3 %collective-permute-start.16 = (f32[4,18,18,1]{2,0,3,1:T(4,128)S(1)}, f32[4,18,18,1]{2,0,3,1:T(4,128)S(1)}, u32[]{:S(2)}, u32[]{:S(2)}) collective-permute-start(f32[4,18,18,1]{2,0,3,1:T(4,128)S(1)} %copy.612), channel_id=1, source_target_pairs={{1,0},{3,2},{5,4},{7,6},{9,8},{11,10},{13,12},{15,14},{17,16},{19,... | collective-permute-start | bytes 15560 | tf_op jit(solution)/shard_map/ppermute | solution.py:19
  103.8 12.6 %collective-permute-start.17 = (f32[4,18,18,1]{2,0,3,1:T(4,128)S(1)}, f32[4,18,18,1]{2,0,3,1:T(4,128)S(1)}, u32[]{:S(2)}, u32[]{:S(2)}) collective-permute-start(f32[4,18,18,1]{2,0,3,1:T(4,128)S(1)} %copy.614), channel_id=1, source_target_pairs={{0,1},{2,3},{4,5},{6,7},{8,9},{10,11},{12,13},{14,15},{16,17},{18,... | collective-permute-start | bytes 15560 | tf_op jit(solution)/shard_map/ppermute | solution.py:18
  124.7 101.5 %collective-permute-start.19 = (f32[4,1,16,128]{3,2,1,0:T(8,128)}, f32[4,1,16,128]{3,2,1,0:T(8,128)}, u32[]{:S(2)}, u32[]{:S(2)}) collective-permute-start(f32[4,1,16,128]{3,2,1,0:T(8,128)} %get-tuple-element.18), channel_id=1, source_target_pairs={{0,8},{8,16},{16,24},{24,32},{32,40},{40,48},{48,56},{56,64},{64,7... | collective-permute-start | bytes 98312 | tf_op jit(solution)/shard_map/ppermute | solution.py:18
  124.9 101.4 %collective-permute-start.18 = (f32[4,1,16,128]{3,2,1,0:T(8,128)}, f32[4,1,16,128]{3,2,1,0:T(8,128)}, u32[]{:S(2)}, u32[]{:S(2)}) collective-permute-start(f32[4,1,16,128]{3,2,1,0:T(8,128)} %get-tuple-element.19), channel_id=1, source_target_pairs={{8,0},{16,8},{24,16},{32,24},{40,32},{48,40},{56,48},{64,56},{72,6... | collective-permute-start | bytes 98312 | tf_op jit(solution)/shard_map/ppermute | solution.py:19
  231.9 18.4 %collective-permute-start.21 = (f32[4,1,16,128]{3,2,1,0:T(8,128)S(1)}, f32[4,1,16,128]{3,2,1,0:T(8,128)S(1)}, u32[]{:S(2)}, u32[]{:S(2)}) collective-permute-start(f32[4,1,16,128]{3,2,1,0:T(8,128)S(1)} %get-tuple-element.16), channel_id=1, source_target_pairs={{0,8},{8,16},{16,24},{24,32},{32,40},{40,48},{48,56},{56,64},{64,7... | collective-permute-start | bytes 98312 | tf_op jit(solution)/shard_map/ppermute | solution.py:18
  232.2 18.1 %collective-permute-start.20 = (f32[4,1,16,128]{3,2,1,0:T(8,128)S(1)}, f32[4,1,16,128]{3,2,1,0:T(8,128)}, u32[]{:S(2)}, u32[]{:S(2)}) collective-permute-start(f32[4,1,16,128]{3,2,1,0:T(8,128)S(1)} %get-tuple-element.17), channel_id=1, source_target_pairs={{8,0},{16,8},{24,16},{32,24},{40,32},{48,40},{56,48},{64,56},{72,6... | collective-permute-start | bytes 98312 | tf_op jit(solution)/shard_map/ppermute | solution.py:19
  258.5 55.1 %collective-permute-start.23 = (f32[4,1,16,128]{3,2,1,0:T(8,128)}, f32[4,1,16,128]{3,2,1,0:T(8,128)S(1)}, u32[]{:S(2)}, u32[]{:S(2)}) collective-permute-start(f32[4,1,16,128]{3,2,1,0:T(8,128)} %get-tuple-element.14), channel_id=1, source_target_pairs={{0,8},{8,16},{16,24},{24,32},{32,40},{40,48},{48,56},{56,64},{64,7... | collective-permute-start | bytes 98312 | tf_op jit(solution)/shard_map/ppermute | solution.py:18
  258.5 55.1 %collective-permute-start.22 = (f32[4,1,16,128]{3,2,1,0:T(8,128)}, f32[4,1,16,128]{3,2,1,0:T(8,128)}, u32[]{:S(2)}, u32[]{:S(2)}) collective-permute-start(f32[4,1,16,128]{3,2,1,0:T(8,128)} %get-tuple-element.15), channel_id=1, source_target_pairs={{8,0},{16,8},{24,16},{32,24},{40,32},{48,40},{56,48},{64,56},{72,6... | collective-permute-start | bytes 98312 | tf_op jit(solution)/shard_map/ppermute | solution.py:19
  372.6 98.3 %all-to-all-start = ((f32[32,1,4,8192]{3,2,1,0:T(4,128)}), f32[32,1,4,8192]{3,2,1,0:T(4,128)}, u32[]{:S(2)}, u32[]{:S(2)}) async-start(f32[32,1,4,8192]{3,2,1,0:T(4,128)} %stack.183), calls=%async_computation | async-start | bytes 8388608 | tf_op jit(solution)/shard_map/all_to_all | solution.py:126
  (26 other events, 89.0 us)
Sparse Core Ops, SparseCore 0:
  45.5 81.0 all-gather.13
  129.2 80.1 all-gather.11
  211.9 80.3 all-gather.9
